TPU v7x, 128 devices: a whole 4x4x4 slice. The times are simulated.
128 devices in a mesh: section: 2 (over y_hi), row: 8 (over z, core), tp: 8 (over x, y_lo).
Axes of the slice: x: 4, y: 4 (y_hi: 2, y_lo: 2; y = y_hi * 2 + y_lo), z: 4, core: 2. Of those that a mesh axis runs over, the one named last changes fastest.
Arguments:
- section_feeds: bfloat16 [2, 2, 128, 8192], P('section', None, None, 'row'), may hold values from -6 to 6
- norm_gain: float32 [2, 8192], P('section', 'row'), may hold values from 0.1 to 1.9
- up_weight: bfloat16 [2, 8192, 32768], P('section', 'row', 'tp'), may hold values from -0.0625 to 0.0625
- down_weight: bfloat16 [2, 32768, 8192], P('section', 'tp', 'row'), may hold values from -0.03125 to 0.03125
Outputs:
- section_ends: bfloat16 [2, 2, 128, 8192], P('section', None, None, 'row')
All inputs are finite; a program needn't handle non-finite values.
Results may differ from a plain program's by a relative error of at most 0.011.
Values may be sent and summed in bfloat16 or wider, within the bound.
No kernel may reach another device: no remote copies, remote signals or barrier semaphores. Data moves between devices by JAX's collectives and lax.ppermute only.
A program may use at most 128 MiB of HBM per device.

v0:
```python
import jax
import jax.numpy as jnp
from jax import lax
from jax.sharding import PartitionSpec as P

D = 8192
epsilon = 1e-05
gelu_coeff = 0.7978845608028654


def shifted(array, axis, by):
    devices = lax.axis_size(axis)
    pairs = [(i, i + by) for i in range(devices) if 0 <= i + by < devices]
    return lax.ppermute(array, axis, pairs)


def gelu_value(inputs):
    inner = gelu_coeff * (inputs + 0.044715 * inputs * inputs * inputs)
    return 0.5 * inputs * (1.0 + jnp.tanh(inner))


def gelu_slope(inputs):
    inner = gelu_coeff * (inputs + 0.044715 * inputs * inputs * inputs)
    tangent = jnp.tanh(inner)
    return 0.5 * (1.0 + tangent) + 0.5 * inputs * (1.0 - tangent * tangent) * gelu_coeff * (
        1.0 + 3.0 * 0.044715 * inputs * inputs
    )


def row_pair(first_arr, second_arr):
    return lax.psum((jnp.sum(first_arr, axis=1), jnp.sum(second_arr, axis=1)), "row")


def cross_section(produced, offset_by):
    return shifted(produced, "section", offset_by)


def body(section_feeds, norm_gain, up_weight, down_weight):
    up_local = up_weight[0]
    down_local = down_weight[0]
    gain_row = norm_gain[0]
    feeds_local = section_feeds[0]
    micro_count = feeds_local.shape[0]
    row_count = feeds_local.shape[1]
    width_local = up_local.shape[0]
    hidden_local = up_local.shape[1]
    is_first = lax.axis_index("section") == 0

    def hidden_side(make_term):
        return lax.psum(make_term(0, hidden_local), "row")

    def hidden_contract(activated, fold_step):
        initial = jnp.zeros((row_count, width_local), jnp.float32)
        return fold_step(initial, activated, 0)

    def feature_total(partial_value):
        return lax.psum(partial_value, "tp")

    def pick_saved(early_item, late_item):
        return jnp.where(is_first, early_item, late_item)

    zeros_full = jnp.zeros((row_count, width_local), jnp.bfloat16)
    saved_list = []
    output_parts = []
    received = zeros_full
    for tick_index in range(micro_count + 1):
        feed_rows = feeds_local[min(tick_index, micro_count - 1)]
        arriving = zeros_full if tick_index == 0 else received
        inputs = jnp.where(is_first, feed_rows, arriving)
        values = inputs.astype(jnp.float32)
        row_sum, squares = row_pair(values, values * values)
        row_mean = row_sum / D
        variance = squares / D - row_mean * row_mean
        forward_inv_std = lax.rsqrt(variance + epsilon)
        forward_normed = (values - row_mean[:, None]) * forward_inv_std[:, None]
        scaled = (forward_normed * gain_row[None, :]).astype(jnp.bfloat16)

        def up_term(offset, length):
            return lax.dot_general(
                up_local, scaled, (((0,), (1,)), ((), ())), preferred_element_type=jnp.float32
            )

        forward_hidden_pre = hidden_side(up_term)
        forward_activated = gelu_value(forward_hidden_pre).astype(jnp.bfloat16)

        def forward_fold(running, shard_part, offset):
            return lax.dot_general(
                shard_part, down_local, (((0,), (0,)), ((), ())), preferred_element_type=jnp.float32
            )

        branch = feature_total(hidden_contract(forward_activated, forward_fold))
        produced = (values + branch).astype(jnp.bfloat16)
        produced, saved = (produced, (forward_normed, forward_inv_std, forward_hidden_pre))
        saved_list.append(saved)
        if tick_index >= 1:
            output_parts.append(produced)
        if tick_index < micro_count:
            received = cross_section(produced, 1)
    grad_parts = []
    for tick_index in range(micro_count + 1):
        feed_rows = feeds_local[min(tick_index, micro_count - 1)]
        arriving = zeros_full if tick_index == 0 else received
        incoming = jnp.where(is_first, arriving, feed_rows)
        early_saved = saved_list[max(tick_index - 1, 0)]
        late_saved = saved_list[min(tick_index + 1, micro_count)]
        saved = jax.tree.map(pick_saved, early_saved, late_saved)
        normed, inv_std, hidden_pre = saved

        def back_term(offset, length):
            return lax.dot_general(
                down_local, incoming, (((1,), (1,)), ((), ())), preferred_element_type=jnp.float32
            )

        hidden_grad = hidden_side(back_term)
        pre_grad = (hidden_grad * gelu_slope(hidden_pre)).astype(jnp.bfloat16)

        def backward_fold(running, shard_part, offset):
            return lax.dot_general(
                shard_part, up_local, (((0,), (1,)), ((), ())), preferred_element_type=jnp.float32
            )

        normed_grad = feature_total(hidden_contract(pre_grad, backward_fold)) * gain_row[None, :]
        first_sum, second_sum = row_pair(normed_grad, normed_grad * normed)
        first_mean = first_sum / D
        second_mean = second_sum / D
        result = incoming.astype(jnp.float32) + inv_std[:, None] * (
            normed_grad - first_mean[:, None] - normed * second_mean[:, None]
        )
        produced = result.astype(jnp.bfloat16)
        if tick_index >= 1:
            grad_parts.append(produced)
        if tick_index < micro_count:
            received = cross_section(produced, -1)
    ends_local = jnp.stack(
        [
            jnp.where(is_first, grad_parts[index_value], output_parts[index_value])
            for index_value in range(micro_count)
        ]
    )
    return ends_local[None]


def solution(mesh):
    placed = (
        P("section", None, None, "row"),
        P("section", "row"),
        P("section", "row", "tp"),
        P("section", "tp", "row"),
    )
    return jax.shard_map(
        body, mesh=mesh, in_specs=placed, out_specs=P("section", None, None, "row"), check_vma=False
    )
```

profile of v0, /device:TPU:1, one launch (start us, length us, event | category | flops | bytes accessed | tf_op | source)
XLA Modules:
  0.0 769.2 jit_solution(4571806862936527683)
XLA Ops:
  8.7 14.5 %all-reduce.6 = (f32[128]{0:T(128)S(1)}, f32[128]{0:T(128)S(1)}) all-reduce(f32[128]{0:T(128)S(1)} %fusion.117, f32[128]{0:T(128)S(1)} %convert_reduce_fusion.2), channel_id=1, replica_groups=mesh['section'=2,'row'=8,'tp'=8] {'row'}, use_global_device_ids=true, to_apply=%region_1.2 | all-reduce | flops 256 | bytes 2048 | tf_op jit(solution)/shard_map/psum | solution.py:31
  23.2 6.2 fusion.24
  29.5 65.3 %all-reduce.18.cloned.1.call-done = f32[4096,128]{0,1:T(8,128)} async-done(((f32[4096,128]{0,1:T(8,128)}), f32[4096,128]{0,1:T(8,128)}) %all-reduce.18.cloned.1.call-update) | async-done | bytes 2097168 | tf_op jit(solution)/shard_map/psum | solution.py:50
  94.8 6.4 fusion.10
  101.3 70.9 %all-reduce.20.cloned.1.call-done = f32[128,1024]{1,0:T(8,128)} async-done(((f32[128,1024]{1,0:T(8,128)}), f32[128,1024]{1,0:T(8,128)}) %all-reduce.20.cloned.1.call-update) | async-done | bytes 524304 | tf_op jit(solution)/shard_map/psum | solution.py:57
  173.3 4.6 collective-permute-start
  177.9 7.7 fusion.33
  185.8 17.8 %all-reduce.5 = (f32[128]{0:T(128)S(1)}, f32[128]{0:T(128)S(1)}) all-reduce(f32[128]{0:T(128)S(1)} %get-tuple-element.14, f32[128]{0:T(128)S(1)} %get-tuple-element.13), channel_id=1, replica_groups=mesh['section'=2,'row'=8,'tp'=8] {'row'}, use_global_device_ids=true, to_apply=%region_7.8 | all-reduce | flops 256 | bytes 2048 | tf_op jit(solution)/shard_map/psum | solution.py:31
  203.5 6.1 fusion.27
  209.7 66.3 %all-reduce.32.cloned.1.call-done = (f32[4096,128]{0,1:T(8,128)}, f32[4096,128]{0,1:T(8,128)}) async-done(((f32[4096,128]{0,1:T(8,128)}, f32[4096,128]{0,1:T(8,128)}), (f32[4096,128]{0,1:T(8,128)}, f32[4096,128]{0,1:T(8,128)})) %all-reduce.32.cloned.1.call-update) | async-done | bytes 4194320 | tf_op jit(solution)/shard_map/psum | solution.py:50
  276.0 6.5 fusion.6
  282.5 7.6 fusion.18
  290.2 75.3 %all-reduce.28.cloned.1.call-done = (f32[128,1024]{1,0:T(8,128)}, f32[128,1024]{1,0:T(8,128)}) async-done(((f32[128,1024]{1,0:T(8,128)}, f32[128,1024]{1,0:T(8,128)}), (f32[128,1024]{1,0:T(8,128)}, f32[128,1024]{1,0:T(8,128)})) %all-reduce.28.cloned.1.call-update) | async-done | bytes 1048592 | tf_op jit(solution)/shard_map/psum | solution.py:57
  366.6 4.8 collective-permute-start.2
  371.4 3.1 collective-permute-done.2
  376.0 17.5 %all-reduce.4 = (f32[128]{0:T(128)S(1)}, f32[128]{0:T(128)S(1)}, f32[128]{0:T(128)S(1)}, f32[128]{0:T(128)S(1)}) all-reduce(f32[128]{0:T(128)S(1)} %get-tuple-element.43, f32[128]{0:T(128)S(1)} %get-tuple-element.44, f32[128]{0:T(128)S(1)} %get-tuple-element.10, ...), channel_id=1, replica_groups=mesh['section'=2,'row'=8,'tp'=8] {'row'}, use_global_device_ids=true, to_apply=%region_19.20 | all-reduce | flops 512 | bytes 4096 | tf_op jit(solution)/shard_map/psum | solution.py:31
  395.2 6.1 fusion.30
  401.3 3.5 collective-permute-done.1
  404.9 7.6 fusion.36
  412.5 66.9 %all-reduce.30.cloned.1.call-done = (f32[4096,128]{0,1:T(8,128)}, f32[4096,128]{0,1:T(8,128)}) async-done(((f32[4096,128]{0,1:T(8,128)}, f32[4096,128]{0,1:T(8,128)}), (f32[4096,128]{0,1:T(8,128)}, f32[4096,128]{0,1:T(8,128)})) %all-reduce.30.cloned.1.call-update) | async-done | bytes 4194320 | tf_op jit(solution)/shard_map/psum | solution.py:50
  479.4 8.6 %fusion.14 = f32[128,1024]{1,0:T(8,128)} fusion(bf16[1,1024,4096]{2,1,0:T(8,128)(2,1)} %param.6, f32[4096,128]{0,1:T(8,128)} %get-tuple-element.32, f32[4096,128]{0,1:T(8,128)} %all-reduce.18.cloned.1.call-done, f32[4096,128]{0,1:T(8,128)} %get-tuple-element.31, pred[]{:T(512)S(6)} %eq.3), kind=kOutput, calls=%fused_computation.14 | convolution fusion | flops 1084227584 | bytes 15204353 | tf_op jit(solution)/shard_map/dot_general | solution.py:118
  488.1 71.2 %all-reduce.22.cloned.1.call-done = f32[128,1024]{1,0:T(8,128)} async-done(((f32[128,1024]{1,0:T(8,128)}), f32[128,1024]{1,0:T(8,128)}) %all-reduce.22.cloned.1.call-update) | async-done | bytes 524304 | tf_op jit(solution)/shard_map/psum | solution.py:57
  560.7 17.7 %all-reduce.3 = (f32[128]{0:T(128)S(1)}, f32[128]{0:T(128)S(1)}) all-reduce(f32[128]{0:T(128)S(1)} %get-tuple-element.8, f32[128]{0:T(128)S(1)} %get-tuple-element.7), channel_id=1, replica_groups=mesh['section'=2,'row'=8,'tp'=8] {'row'}, use_global_device_ids=true, to_apply=%region_28.29 | all-reduce | flops 256 | bytes 2048 | tf_op jit(solution)/shard_map/psum | solution.py:31
  578.4 1.5 select_bitcast_fusion
  581.2 9.4 %collective-permute-done.3 = bf16[128,1024]{1,0:T(8,128)(2,1)S(1)} collective-permute-done((bf16[128,1024]{1,0:T(8,128)(2,1)S(1)}, bf16[128,1024]{1,0:T(8,128)(2,1)S(1)}, u32[]{:S(2)}, u32[]{:S(2)}) %collective-permute-start.3) | collective-permute-done | bytes 262176 | tf_op jit(solution)/shard_map/ppermute | solution.py:14
  590.6 7.6 fusion.39
  598.5 6.5 fusion
  605.0 52.8 %all-reduce.24.cloned.1.call-done = f32[4096,128]{0,1:T(8,128)} async-done(((f32[4096,128]{0,1:T(8,128)}), f32[4096,128]{0,1:T(8,128)}) %all-reduce.24.cloned.1.call-update) | async-done | bytes 2097168 | tf_op jit(solution)/shard_map/psum | solution.py:50
  657.9 8.7 %fusion.12 = f32[128,1024]{1,0:T(8,128)} fusion(bf16[1,1024,4096]{2,1,0:T(8,128)(2,1)} %param.6, f32[4096,128]{0,1:T(8,128)} %all-reduce.24.cloned.1.call-done, f32[4096,128]{0,1:T(8,128)} %get-tuple-element.33, f32[4096,128]{0,1:T(8,128)} %get-tuple-element.31, pred[]{:T(512)S(6)} %eq.3), kind=kOutput, calls=%fused_computation.12 | convolution fusion | flops 1084227584 | bytes 15204353 | tf_op jit(solution)/shard_map/dot_general | solution.py:118
  666.5 75.1 %all-reduce.26.cloned.1.call-done = (f32[128,1024]{1,0:T(8,128)}, f32[128,1024]{1,0:T(8,128)}) async-done(((f32[128,1024]{1,0:T(8,128)}, f32[128,1024]{1,0:T(8,128)}), (f32[128,1024]{1,0:T(8,128)}, f32[128,1024]{1,0:T(8,128)})) %all-reduce.26.cloned.1.call-update) | async-done | bytes 1048592 | tf_op jit(solution)/shard_map/psum | solution.py:57
  743.0 16.8 %all-reduce.2 = (f32[128]{0:T(128)S(1)}, f32[128]{0:T(128)S(1)}) all-reduce(f32[128]{0:T(128)S(1)} %get-tuple-element.6, f32[128]{0:T(128)S(1)} %get-tuple-element.5), channel_id=1, replica_groups=mesh['section'=2,'row'=8,'tp'=8] {'row'}, use_global_device_ids=true, to_apply=%region_34.35 | all-reduce | flops 256 | bytes 2048 | tf_op jit(solution)/shard_map/psum | solution.py:31
  759.9 1.6 fusion.151
  (50 shorter events, 13.4 us)
Async XLA Ops:
  6.5 88.3 %all-reduce.18.cloned.1.call-start = ((), (), s32[]{:S(2)}) async-start(), calls=%async_computation | async-start | bytes 4194304 | tf_op jit(solution)/shard_map/psum | solution.py:50
  29.4 142.7 %copy-start = (bf16[1,2,128,1024]{3,2,1,0:T(8,128)(2,1)S(1)}, bf16[1,2,128,1024]{3,2,1,0:T(8,128)(2,1)}, u32[]{:S(2)}) copy-start(bf16[1,2,128,1024]{3,2,1,0:T(8,128)(2,1)} %param.4) | copy-start | bytes 1572868
  29.4 142.7 %all-reduce.20.cloned.1.call-start = ((), (), s32[]{:S(2)}) async-start(), calls=%async_computation.1 | async-start | bytes 1048576 | tf_op jit(solution)/shard_map/psum | solution.py:57
  101.2 174.8 %all-reduce.32.cloned.1.call-start = ((), (), s32[]{:S(2)}) async-start(), calls=%async_computation.7 | async-start | bytes 8388608 | tf_op jit(solution)/shard_map/psum | solution.py:50
  173.3 30.3 %copy-start.2 = (f32[1,1024]{1,0:T(1,128)S(1)}, f32[1,1024]{1,0:T(1,128)}, u32[]{:S(2)}) copy-start(f32[1,1024]{1,0:T(1,128)} %param.5) | copy-start | bytes 12292
  173.3 12.3 %collective-permute-start = (bf16[128,1024]{1,0:T(8,128)(2,1)S(1)}, bf16[128,1024]{1,0:T(8,128)(2,1)S(1)}, u32[]{:S(2)}, u32[]{:S(2)}) collective-permute-start(bf16[128,1024]{1,0:T(8,128)(2,1)S(1)} %fusion.118), channel_id=1, source_target_pairs={{0,64},{1,65},{2,66},{3,67},{4,68},{5,69},{6,70},{7,71},{8,72},{9,... | collective-permute-start | bytes 786440 | tf_op jit(solution)/shard_map/ppermute | solution.py:14
  209.6 155.8 %all-reduce.28.cloned.1.call-start = ((), (), s32[]{:S(2)}) async-start(), calls=%async_computation.5 | async-start | bytes 2097152 | tf_op jit(solution)/shard_map/psum | solution.py:57
  276.0 6.5 copy-start.3
  276.0 6.5 copy-start.4
  276.0 6.5 copy-start.5
  290.1 189.3 %all-reduce.30.cloned.1.call-start = ((), (), s32[]{:S(2)}) async-start(), calls=%async_computation.6 | async-start | bytes 8388608 | tf_op jit(solution)/shard_map/psum | solution.py:50
  365.4 28.1 %copy-start.1 = (f32[128,1024]{1,0:T(8,128)S(1)}, f32[128,1024]{1,0:T(8,128)}, u32[]{:S(2)}) copy-start(f32[128,1024]{1,0:T(8,128)} %get-tuple-element.18) | copy-start | bytes 1572868
  366.6 7.9 %collective-permute-start.2 = (bf16[128,1024]{1,0:T(8,128)(2,1)S(1)}, bf16[128,1024]{1,0:T(8,128)(2,1)S(1)}, u32[]{:S(2)}, u32[]{:S(2)}) collective-permute-start(bf16[128,1024]{1,0:T(8,128)(2,1)S(1)} %fusion.130), channel_id=1, source_target_pairs={{0,64},{1,65},{2,66},{3,67},{4,68},{5,69},{6,70},{7,71},{8,72},{9,... | collective-permute-start | bytes 786440 | tf_op jit(solution)/shard_map/ppermute | solution.py:14
  393.9 11.0 %collective-permute-start.1 = (bf16[128,1024]{1,0:T(8,128)(2,1)S(1)}, bf16[128,1024]{1,0:T(8,128)(2,1)S(1)}, u32[]{:S(2)}, u32[]{:S(2)}) collective-permute-start(bf16[128,1024]{1,0:T(8,128)(2,1)S(1)} %add_convert_fusion.2), channel_id=1, source_target_pairs={{64,0},{65,1},{66,2},{67,3},{68,4},{69,5},{70,6},{71,7},{72,8},{73... | collective-permute-start | bytes 786440 | tf_op jit(solution)/shard_map/ppermute | solution.py:14
  412.5 146.8 %all-reduce.22.cloned.1.call-start = ((), (), s32[]{:S(2)}) async-start(), calls=%async_computation.2 | async-start | bytes 1048576 | tf_op jit(solution)/shard_map/psum | solution.py:57
  488.1 169.8 %all-reduce.24.cloned.1.call-start = ((), (), s32[]{:S(2)}) async-start(), calls=%async_computation.3 | async-start | bytes 4194304 | tf_op jit(solution)/shard_map/psum | solution.py:50
  579.9 10.7 %collective-permute-start.3 = (bf16[128,1024]{1,0:T(8,128)(2,1)S(1)}, bf16[128,1024]{1,0:T(8,128)(2,1)S(1)}, u32[]{:S(2)}, u32[]{:S(2)}) collective-permute-start(bf16[128,1024]{1,0:T(8,128)(2,1)S(1)} %get-tuple-element.36), channel_id=1, source_target_pairs={{64,0},{65,1},{66,2},{67,3},{68,4},{69,5},{70,6},{71,7},{72,8},{73... | collective-permute-start | bytes 786440 | tf_op jit(solution)/shard_map/ppermute | solution.py:14
  598.3 143.4 %all-reduce.26.cloned.1.call-start = ((), (), s32[]{:S(2)}) async-start(), calls=%async_computation.4 | async-start | bytes 2097152 | tf_op jit(solution)/shard_map/psum | solution.py:57
Sparse Core Ops, SparseCore 0:
  29.5 65.2 all-reduce.17
  101.3 70.7 all-reduce.19
  209.7 66.2 all-reduce.31
  290.2 75.1 all-reduce.27
  412.6 66.7 all-reduce.29
  488.2 71.0 all-reduce.21
  598.4 59.4 all-reduce.23
  666.7 74.9 all-reduce.25
where the time goes:
time: 770 us; the launch traced here: 769 us
  waiting for transfers between devices  560 us (73%)
  matrix products  85.5 us (11%)
  blocking collectives  84.3 us (11%)
  between operations  13.6 us (2%)
  other arithmetic  13.3 us (2%)
  starting transfers between devices  12.5 us (2%)
    psum x4, waiting for transfers between devices, feature_total(): return lax.psum(partial_value, 'tp')  292 us
    psum x4, waiting for transfers between devices, hidden_side(): return lax.psum(make_term(0, hidden_local), 'row')  251 us
    psum x5, blocking collectives, row_pair(): lax.psum((jnp.sum(first_arr, axis=1), jnp.sum(second_arr, axis=1)), 'row')  84.3 us
    dot_general x3, matrix products, backward_fold(): lax.dot_general(shard_part, up_local, (((0,), (1,)), ((), ())), preferred...  24.9 us
    dot_general x3, matrix products, back_term(): lax.dot_general(down_local, incoming, (((1,), (1,)), ((), ())), preferred...  22.9 us
    dot_general x3, matrix products, forward_fold(): lax.dot_general(shard_part, down_local, (((0,), (0,)), ((), ())), preferr...  19.4 us
    dot_general x3, matrix products, up_term(): lax.dot_general(up_local, scaled, (((0,), (1,)), ((), ())), preferred_ele...  18.4 us
    ppermute x4, waiting for transfers between devices, shifted(): return lax.ppermute(array, axis, pairs)  16 us
  transfers between devices with their start and end apart: 12, of which 11 were waited for; matrix products, arithmetic and copies ran while one was open for 3% of the time, Pallas kernels for 0%

commit v1 on v0

--- a/solution.py
+++ b/solution.py
@@ -47,7 +47,7 @@
     is_first = lax.axis_index("section") == 0
 
     def hidden_side(make_term):
-        return lax.psum(make_term(0, hidden_local), "row")
+        return jnp.sum(lax.all_gather(make_term(0, hidden_local), "row"), axis=0)
 
     def hidden_contract(activated, fold_step):
         initial = jnp.zeros((row_count, width_local), jnp.float32)

time: 770 us -> 1070 us (1.39)
  waiting for transfers between devices: 560 us -> 720 us
  local copies, waits for them, and re-layouts: 0.03 us -> 99.7 us
  other arithmetic: 13.3 us -> 54.6 us
    all_gather x0 -> x6, waiting for transfers between devices: none -> 416 us  [hidden_side(): return jnp.sum(lax.all_gather(make_term(0, hidden_local), 'row'), axis=0)]
    psum x4 -> x0, waiting for transfers between devices: 251 us -> none  [hidden_side(): return lax.psum(make_term(0, hidden_local), 'row')]
    unnamed x12 -> x30, local copies, waits for them, and re-layouts: 0.03 us -> 99.7 us
    reduce_sum x0 -> x5, other arithmetic: none -> 39.7 us  [hidden_side(): return jnp.sum(lax.all_gather(make_term(0, hidden_local), 'row'), axis=0)]
    psum x4, waiting for transfers between devices: 292 us -> 279 us  [feature_total(): return lax.psum(partial_value, 'tp')]
  transfers between devices with their start and end apart: 12 -> 14, of which waited for: 11 -> 14; matrix products, arithmetic and copies ran while one was open for 3% -> 7% of each run, Pallas kernels for 0% -> 0%
where the time goes in v1:
time: 1070 us; the launch traced here: 1060 us
  waiting for transfers between devices  720 us (67%)
  local copies, waits for them, and re-layouts  99.7 us (9%)
  blocking collectives  85.9 us (8%)
  matrix products  76.2 us (7%)
  other arithmetic  54.6 us (5%)
  between operations  14.2 us (1%)
  starting transfers between devices  11.8 us (1%)
    all_gather x6, waiting for transfers between devices, hidden_side(): return jnp.sum(lax.all_gather(make_term(0, hidden_local), 'row'), axis=0)  416 us
    psum x4, waiting for transfers between devices, feature_total(): return lax.psum(partial_value, 'tp')  279 us
    unnamed x30, local copies, waits for them, and re-layouts  99.7 us
    psum x5, blocking collectives, row_pair(): lax.psum((jnp.sum(first_arr, axis=1), jnp.sum(second_arr, axis=1)), 'row')  85.9 us
    reduce_sum x5, other arithmetic, hidden_side(): return jnp.sum(lax.all_gather(make_term(0, hidden_local), 'row'), axis=0)  39.7 us
    ppermute x4, waiting for transfers between devices, shifted(): return lax.ppermute(array, axis, pairs)  25.8 us
    dot_general x3, matrix products, back_term(): lax.dot_general(down_local, incoming, (((1,), (1,)), ((), ())), preferred...  23.1 us
  transfers between devices with their start and end apart: 14, of which 14 were waited for; matrix products, arithmetic and copies ran while one was open for 7% of the time, Pallas kernels for 0%

profile of v1, /device:TPU:1, one launch (start us, length us, event | category | flops | bytes accessed | tf_op | source)
XLA Modules:
  0.0 1062.8 jit_solution(16173544891787397443)
XLA Ops:
  8.7 14.5 %all-reduce.6 = (f32[128]{0:T(128)S(1)}, f32[128]{0:T(128)S(1)}) all-reduce(f32[128]{0:T(128)S(1)} %fusion.117, f32[128]{0:T(128)S(1)} %convert_reduce_fusion.2), channel_id=1, replica_groups=mesh['section'=2,'row'=8,'tp'=8] {'row'}, use_global_device_ids=true, to_apply=%region_1.2 | all-reduce | flops 256 | bytes 2048 | tf_op jit(solution)/shard_map/psum | solution.py:31
  23.2 6.2 fusion.24
  29.5 86.8 %all-gather.13.cloned.1.call-done = f32[32768,128]{0,1:T(8,128)} async-done(((f32[4096,128]{0,1:T(8,128)}), f32[32768,128]{0,1:T(8,128)}) %all-gather.13.cloned.1.call-update) | async-done | bytes 16777232 | tf_op jit(solution)/shard_map/all_gather | solution.py:50
  116.3 15.5 %copy.5 = f32[16,8,8,4096]{3,2,1,0:T(8,128)S(1)} copy(f32[16,8,8,4096]{3,1,2,0:T(8,128)} %bitcast.144) | data formatting | bytes 33554432
  142.9 7.6 fusion.33
  150.6 61.8 %all-reduce.12.cloned.1.call-done = f32[128,1024]{1,0:T(8,128)} async-done(((f32[128,1024]{1,0:T(8,128)}), f32[128,1024]{1,0:T(8,128)}) %all-reduce.12.cloned.1.call-update) | async-done | bytes 524304 | tf_op jit(solution)/shard_map/psum | solution.py:57
  221.6 19.0 %all-reduce.5 = (f32[128]{0:T(128)S(1)}, f32[128]{0:T(128)S(1)}) all-reduce(f32[128]{0:T(128)S(1)} %get-tuple-element.14, f32[128]{0:T(128)S(1)} %get-tuple-element.13), channel_id=1, replica_groups=mesh['section'=2,'row'=8,'tp'=8] {'row'}, use_global_device_ids=true, to_apply=%region_7.8 | all-reduce | flops 256 | bytes 2048 | tf_op jit(solution)/shard_map/psum | solution.py:31
  240.7 6.3 fusion.27
  247.0 57.4 %all-gather.15.cloned.1.call-done = f32[32768,128]{0,1:T(8,128)} async-done(((f32[4096,128]{0,1:T(8,128)}), f32[32768,128]{0,1:T(8,128)}) %all-gather.15.cloned.1.call-update) | async-done | bytes 16777232 | tf_op jit(solution)/shard_map/all_gather | solution.py:50
  304.4 18.0 %copy.6 = f32[16,8,8,4096]{3,2,1,0:T(8,128)} copy(f32[16,8,8,4096]{3,1,2,0:T(8,128)} %bitcast.139) | data formatting | bytes 33554432
  322.4 69.2 %all-gather.17.cloned.1.call-done = f32[32768,128]{0,1:T(8,128)} async-done(((f32[4096,128]{0,1:T(8,128)}), f32[32768,128]{0,1:T(8,128)}) %all-gather.17.cloned.1.call-update) | async-done | bytes 16777232 | tf_op jit(solution)/shard_map/all_gather | solution.py:50
  391.7 17.8 %copy.7 = f32[16,8,8,4096]{3,2,1,0:T(8,128)} copy(f32[16,8,8,4096]{3,1,2,0:T(8,128)} %bitcast.142) | data formatting | bytes 33554432
  409.5 17.0 %bitcast_reduce_fusion.3 = (f32[4096,128]{0,1:T(8,128)S(1)}, f32[4096,128]{0,1:T(8,128)}) fusion(f32[16,8,8,4096]{3,2,1,0:T(8,128)} %copy.7, f32[16,8,8,4096]{3,2,1,0:T(8,128)} %copy.6), kind=kLoop, calls=%fused_computation.3 | loop fusion | flops 7340032 | bytes 37748736 | tf_op jit(solution)/shard_map/reduce_sum | solution.py:50
  434.7 73.7 %all-reduce.18.cloned.1.call-done = (f32[128,1024]{1,0:T(8,128)}, f32[128,1024]{1,0:T(8,128)}) async-done(((f32[128,1024]{1,0:T(8,128)}, f32[128,1024]{1,0:T(8,128)}), (f32[128,1024]{1,0:T(8,128)}, f32[128,1024]{1,0:T(8,128)})) %all-reduce.18.cloned.1.call-update) | async-done | bytes 1048592 | tf_op jit(solution)/shard_map/psum | solution.py:57
  518.6 17.9 %all-reduce.4 = (f32[128]{0:T(128)S(1)}, f32[128]{0:T(128)S(1)}, f32[128]{0:T(128)S(1)}, f32[128]{0:T(128)S(1)}) all-reduce(f32[128]{0:T(128)S(1)} %get-tuple-element.39, f32[128]{0:T(128)S(1)} %get-tuple-element.40, f32[128]{0:T(128)S(1)} %get-tuple-element.10, ...), channel_id=1, replica_groups=mesh['section'=2,'row'=8,'tp'=8] {'row'}, use_global_device_ids=true, to_apply=%region_19.20 | all-reduce | flops 512 | bytes 4096 | tf_op jit(solution)/shard_map/psum | solution.py:31
  545.4 9.8 collective-permute-done.1
  555.2 7.9 fusion.36
  563.2 63.3 %all-gather.21.cloned.1.call-done = f32[32768,128]{0,1:T(8,128)} async-done(((f32[4096,128]{0,1:T(8,128)}), f32[32768,128]{0,1:T(8,128)}) %all-gather.21.cloned.1.call-update) | async-done | bytes 16777232 | tf_op jit(solution)/shard_map/all_gather | solution.py:50
  626.6 15.6 %copy.9 = f32[16,8,8,4096]{3,2,1,0:T(8,128)S(1)} copy(f32[16,8,8,4096]{3,1,2,0:T(8,128)} %bitcast.140) | data formatting | bytes 33554432
  642.2 6.7 bitcast_reduce_fusion.1
  648.9 65.1 %all-gather.19.cloned.1.call-done = f32[32768,128]{0,1:T(8,128)} async-done(((f32[4096,128]{0,1:T(8,128)}), f32[32768,128]{0,1:T(8,128)}) %all-gather.19.cloned.1.call-update) | async-done | bytes 16777232 | tf_op jit(solution)/shard_map/all_gather | solution.py:50
  714.0 15.5 %copy.8 = f32[16,8,8,4096]{3,2,1,0:T(8,128)S(1)} copy(f32[16,8,8,4096]{3,1,2,0:T(8,128)} %bitcast.141) | data formatting | bytes 33554432
  735.0 7.4 fusion.14
  742.5 69.5 %all-reduce.14.cloned.1.call-done = f32[128,1024]{1,0:T(8,128)} async-done(((f32[128,1024]{1,0:T(8,128)}), f32[128,1024]{1,0:T(8,128)}) %all-reduce.14.cloned.1.call-update) | async-done | bytes 524304 | tf_op jit(solution)/shard_map/psum | solution.py:57
  813.3 17.7 %all-reduce.3 = (f32[128]{0:T(128)S(1)}, f32[128]{0:T(128)S(1)}) all-reduce(f32[128]{0:T(128)S(1)} %get-tuple-element.8, f32[128]{0:T(128)S(1)} %get-tuple-element.7), channel_id=1, replica_groups=mesh['section'=2,'row'=8,'tp'=8] {'row'}, use_global_device_ids=true, to_apply=%region_28.29 | all-reduce | flops 256 | bytes 2048 | tf_op jit(solution)/shard_map/psum | solution.py:31
  834.5 9.4 collective-permute-done.3
  843.9 7.6 fusion.39
  859.0 73.7 %all-gather.23.cloned.1.call-done = f32[32768,128]{0,1:T(8,128)} async-done(((f32[4096,128]{0,1:T(8,128)}), f32[32768,128]{0,1:T(8,128)}) %all-gather.23.cloned.1.call-update) | async-done | bytes 16777232 | tf_op jit(solution)/shard_map/all_gather | solution.py:50
  932.7 15.7 %copy.10 = f32[16,8,8,4096]{3,2,1,0:T(8,128)S(1)} copy(f32[16,8,8,4096]{3,1,2,0:T(8,128)} %bitcast.143) | data formatting | bytes 33554432
  953.7 7.4 fusion.12
  961.2 73.7 %all-reduce.16.cloned.1.call-done = (f32[128,1024]{1,0:T(8,128)}, f32[128,1024]{1,0:T(8,128)}) async-done(((f32[128,1024]{1,0:T(8,128)}, f32[128,1024]{1,0:T(8,128)}), (f32[128,1024]{1,0:T(8,128)}, f32[128,1024]{1,0:T(8,128)})) %all-reduce.16.cloned.1.call-update) | async-done | bytes 1048592 | tf_op jit(solution)/shard_map/psum | solution.py:57
  1036.2 16.8 %all-reduce.2 = (f32[128]{0:T(128)S(1)}, f32[128]{0:T(128)S(1)}) all-reduce(f32[128]{0:T(128)S(1)} %get-tuple-element.6, f32[128]{0:T(128)S(1)} %get-tuple-element.5), channel_id=1, replica_groups=mesh['section'=2,'row'=8,'tp'=8] {'row'}, use_global_device_ids=true, to_apply=%region_34.35 | all-reduce | flops 256 | bytes 2048 | tf_op jit(solution)/shard_map/psum | solution.py:31
  (82 shorter events, 76.9 us)
Async XLA Ops:
  6.5 109.8 %all-gather.13.cloned.1.call-start = ((), (), s32[]{:S(2)}) async-start(), calls=%async_computation.2 | async-start | bytes 18874368 | tf_op jit(solution)/shard_map/all_gather | solution.py:50
  29.4 183.0 %all-reduce.12.cloned.1.call-start = ((), (), s32[]{:S(2)}) async-start(), calls=%async_computation | async-start | bytes 1048576 | tf_op jit(solution)/shard_map/psum | solution.py:57
  137.1 5.8 copy-start
  142.8 161.6 %all-gather.15.cloned.1.call-start = ((), (), s32[]{:S(2)}) async-start(), calls=%async_computation.3 | async-start | bytes 18874368 | tf_op jit(solution)/shard_map/all_gather | solution.py:50
  150.5 90.2 %copy-start.5 = (f32[1,1024]{1,0:T(1,128)S(1)}, f32[1,1024]{1,0:T(1,128)}, u32[]{:S(2)}) copy-start(f32[1,1024]{1,0:T(1,128)} %param.5) | copy-start | bytes 12292
  150.5 241.1 %all-gather.17.cloned.1.call-start = ((), (), s32[]{:S(2)}) async-start(), calls=%async_computation.4 | async-start | bytes 18874368 | tf_op jit(solution)/shard_map/all_gather | solution.py:50
  213.5 7.9 collective-permute-start
  246.9 261.5 %all-reduce.18.cloned.1.call-start = ((), (), s32[]{:S(2)}) async-start(), calls=%async_computation.9 | async-start | bytes 2097152 | tf_op jit(solution)/shard_map/psum | solution.py:57
  391.7 34.9 %slice-start.2 = ((s8[8388608]{0:T(1024)(128)(4,1)}), s8[4194304]{0:T(1024)(128)(4,1)S(1)}, s32[]{:S(2)}) async-start(s8[8388608]{0:T(1024)(128)(4,1)} %bitcast.137), calls=%async_computation.12 | async-start | bytes 8388608
  391.7 37.3 %slice-start = ((s8[8388608]{0:T(1024)(128)(4,1)}), s8[4194304]{0:T(1024)(128)(4,1)S(1)}, s32[]{:S(2)}) async-start(s8[8388608]{0:T(1024)(128)(4,1)} %bitcast.135), calls=%async_computation.10 | async-start | bytes 8388608
  409.5 17.0 %slice-start.3 = ((s8[8388608]{0:T(1024)(128)(4,1)}), s8[4194304]{0:T(1024)(128)(4,1)S(1)}, s32[]{:S(2)}) async-start(s8[8388608]{0:T(1024)(128)(4,1)} %bitcast.137), calls=%async_computation.13 | async-start | bytes 8388608
  409.5 19.4 %slice-start.1 = ((s8[8388608]{0:T(1024)(128)(4,1)}), s8[4194304]{0:T(1024)(128)(4,1)S(1)}, s32[]{:S(2)}) async-start(s8[8388608]{0:T(1024)(128)(4,1)} %bitcast.135), calls=%async_computation.11 | async-start | bytes 8388608
  426.5 2.4 copy-start.1
  434.7 191.9 %all-gather.21.cloned.1.call-start = ((), (), s32[]{:S(2)}) async-start(), calls=%async_computation.6 | async-start | bytes 18874368 | tf_op jit(solution)/shard_map/all_gather | solution.py:50
  509.5 7.6 copy-start.6
  509.5 7.6 collective-permute-start.2
  542.6 171.4 %all-gather.19.cloned.1.call-start = ((), (), s32[]{:S(2)}) async-start(), calls=%async_computation.5 | async-start | bytes 18874368 | tf_op jit(solution)/shard_map/all_gather | solution.py:50
  544.1 11.1 %collective-permute-start.1 = (bf16[128,1024]{1,0:T(8,128)(2,1)S(1)}, bf16[128,1024]{1,0:T(8,128)(2,1)S(1)}, u32[]{:S(2)}, u32[]{:S(2)}) collective-permute-start(bf16[128,1024]{1,0:T(8,128)(2,1)S(1)} %add_convert_fusion.2), channel_id=1, source_target_pairs={{64,0},{65,1},{66,2},{67,3},{68,4},{69,5},{70,6},{71,7},{72,8},{73... | collective-permute-start | bytes 786440 | tf_op jit(solution)/shard_map/ppermute | solution.py:14
  563.2 248.8 %all-reduce.14.cloned.1.call-start = ((), (), s32[]{:S(2)}) async-start(), calls=%async_computation.1 | async-start | bytes 1048576 | tf_op jit(solution)/shard_map/psum | solution.py:57
  729.5 5.5 copy-start.3
  742.4 190.3 %all-gather.23.cloned.1.call-start = ((), (), s32[]{:S(2)}) async-start(), calls=%async_computation.7 | async-start | bytes 18874368 | tf_op jit(solution)/shard_map/all_gather | solution.py:50
  833.2 10.7 %collective-permute-start.3 = (bf16[128,1024]{1,0:T(8,128)(2,1)S(1)}, bf16[128,1024]{1,0:T(8,128)(2,1)S(1)}, u32[]{:S(2)}, u32[]{:S(2)}) collective-permute-start(bf16[128,1024]{1,0:T(8,128)(2,1)S(1)} %get-tuple-element.32), channel_id=1, source_target_pairs={{64,0},{65,1},{66,2},{67,3},{68,4},{69,5},{70,6},{71,7},{72,8},{73... | collective-permute-start | bytes 786440 | tf_op jit(solution)/shard_map/ppermute | solution.py:14
  851.5 1.6 copy-start.4
  851.5 183.4 %all-reduce.16.cloned.1.call-start = ((), (), s32[]{:S(2)}) async-start(), calls=%async_computation.8 | async-start | bytes 2097152 | tf_op jit(solution)/shard_map/psum | solution.py:57
  948.4 5.3 copy-start.2
  961.1 93.6 %copy-start.7 = (bf16[1,128,1024]{2,1,0:T(8,128)(2,1)S(1)}, bf16[1,128,1024]{2,1,0:T(8,128)(2,1)}, u32[]{:S(2)}) copy-start(bf16[1,128,1024]{2,1,0:T(8,128)(2,1)} %get-tuple-element.31) | copy-start | bytes 786436
Sparse Core Ops, SparseCore 0:
  29.5 86.6 all-gather.12
  143.0 69.3 all-reduce.11
  214.2 90.1 all-gather.14
  306.1 85.5 all-gather.16
  434.8 73.5 all-reduce.17
  542.7 83.7 all-gather.20
  628.4 85.6 all-gather.18
  742.5 69.3 all-reduce.13
  851.6 81.0 all-gather.22
  961.3 73.5 all-reduce.15
